TPU v7x, 32 devices: a whole 2x2x4 slice. The times are simulated.
32 devices in a mesh: win: 2 (over y), tile: 4 (over z), view: 4 (over x, core).
Axes of the slice: x: 2, y: 2, z: 4, core: 2. Of those that a mesh axis runs over, the one named last changes fastest.
Arguments:
- measured: float32 [4, 8, 8, 32, 256], P('view', None, ('win', 'tile')), parts along dimension 2, may hold values from 0.25 to 4
- estimate: float32 [8, 8, 32, 256], P('view', ('win', 'tile')), parts along dimension 1, may hold values from 0.24 to 2.56
- psf_taps: float32 [4, 3, 4, 15], P('view'), may hold values from 0.02 to 0.1
- background: float32 [4], P('view'), may hold values from 0.5 to 3
Outputs:
- updated: float32 [8, 8, 32, 256], P('view', ('win', 'tile')), parts along dimension 1
There are 2 independent parts, one for each index of `win`. A program takes and returns all parts, laid end to end along the dimension named above; an argument that names none is the same for every part. Nothing has to cross between parts.
All inputs are finite; a program needn't handle non-finite values.
Results may differ from a plain program's by a relative error of at most 0.0001.
Values sent between devices are 32-bit elements; how exact they have to be, the bound alone decides.
A program may use at most 64 MiB of HBM per device.

v0:
```python
import jax
import jax.numpy as jnp
from jax import lax
from jax.sharding import PartitionSpec as P

HIGHEST = lax.Precision.HIGHEST


def extended_2(cells, sides, width):
    for axis, dim in sides:
        count = lax.axis_size(axis)
        ends = count - 1
        head = lax.slice_in_dim(cells, 0, width, axis=dim)
        tail = lax.slice_in_dim(cells, cells.shape[dim] - width, cells.shape[dim], axis=dim)
        cells = jnp.concatenate(
            [
                lax.ppermute(tail, axis, [(i, (i + 1) % count) for i in range(ends)]),
                cells,
                lax.ppermute(head, axis, [((i + 1) % count, i) for i in range(ends)]),
            ],
            axis=dim,
        )
    return cells


def banded(kernel, n_out, n_in, pad_in, direction):
    support = kernel.shape[-1]
    out_pos = lax.broadcasted_iota(jnp.int32, (n_out, n_in), 0)
    in_pos = lax.broadcasted_iota(jnp.int32, (n_out, n_in), 1) - pad_in
    tap_index = direction * (in_pos - out_pos) + support // 2
    matrix = jnp.zeros((kernel.shape[0], n_out, n_in), jnp.float32)
    for offset in range(support):
        hit = (tap_index == offset).astype(jnp.float32)
        matrix = matrix + kernel[:, offset][:, None, None] * hit[None]
    return matrix


def plane_pass(volume, matrix_x, matrix_y):
    section = jnp.einsum("ab,zby->zay", matrix_x, volume, precision=HIGHEST)
    return jnp.einsum("zay,cy->zac", section, matrix_y, precision=HIGHEST)


def framed(volume, radius):
    extended = extended_2(volume, (("tile", 1),), radius)
    return jnp.pad(extended, ((0, 0), (0, 0), (radius, radius)))


def shards(measured, estimate, psf_taps, background):
    kernel = psf_taps[0]
    own_slices = estimate[:, 0]
    slice_count, tile_rows, columns = own_slices.shape
    view_count = lax.axis_size("view")
    depth = slice_count * view_count
    support = kernel.shape[-1]
    radius = support // 2
    rank_count = kernel.shape[1]
    forward_x = banded(kernel[1], tile_rows, tile_rows + 2 * radius, radius, 1)
    forward_y = banded(kernel[2], columns, columns + 2 * radius, radius, 1)
    forward_z = banded(kernel[0], depth, depth, 0, 1)
    zeros_tile = jnp.zeros((depth, tile_rows, columns), jnp.float32)
    estimate_rim = framed(own_slices, radius)
    totals = zeros_tile
    block_part = lax.all_gather(estimate_rim, "view", axis=0, tiled=True)
    for add_member in range(rank_count):
        section = plane_pass(block_part, forward_x[add_member], forward_y[add_member])
        chosen = forward_z[add_member]
        totals = totals + jnp.einsum("cz,zay->cay", chosen, section, precision=HIGHEST)
    predicted = totals
    predicted = predicted + background[0]
    quotient = measured[0, :, 0] / predicted
    ratio_rim = framed(quotient, radius)
    adjoint_x = banded(kernel[1], tile_rows, tile_rows + 2 * radius, radius, -1)
    adjoint_y = banded(kernel[2], columns, columns + 2 * radius, radius, -1)
    adjoint_z = banded(kernel[0], depth, depth, 0, -1)
    norm_total = jnp.sum(jnp.prod(jnp.sum(kernel, axis=2), axis=0))
    planes = jnp.stack(
        [
            plane_pass(ratio_rim, adjoint_x[member], adjoint_y[member])
            for member in range(rank_count)
        ]
    )
    correction = lax.psum_scatter(
        jnp.einsum("rcz,rzay->cay", adjoint_z, planes, precision=HIGHEST) / norm_total,
        "view",
        scatter_dimension=0,
        tiled=True,
    )
    return (own_slices * correction / view_count)[:, None]


def solution(mesh):
    return jax.shard_map(
        shards,
        mesh=mesh,
        in_specs=(
            P("view", None, ("win", "tile"), None, None),
            P("view", ("win", "tile"), None, None),
            P("view", None, None, None),
            P("view"),
        ),
        out_specs=P("view", ("win", "tile"), None, None),
        check_vma=False,
    )
```

profile of v0, /device:TPU:0, one launch (start us, length us, event | category | flops | bytes accessed | tf_op | source)
XLA Modules:
  0.0 83.0 jit_solution(12016115702907421253)
XLA Ops:
  6.5 0.7 fusion.266
  7.3 4.9 %collective-permute-start = (f32[2,7,256]{2,1,0:T(8,128)S(1)}, f32[2,7,256]{2,1,0:T(8,128)S(1)}, u32[]{:S(2)}, u32[]{:S(2)}) collective-permute-start(f32[2,7,256]{2,1,0:T(8,128)S(1)} %get-tuple-element.52), channel_id=1, source_target_pairs={{0,4},{4,8},{8,12},{1,5},{5,9},{9,13},{2,6},{6,10},{10,14},{3,7},{... | collective-permute-start | bytes 43016 | tf_op jit(solution)/shard_map/ppermute | solution.py:17
  12.2 1.3 %collective-permute-start.1 = (f32[2,7,256]{2,1,0:T(8,128)S(1)}, f32[2,7,256]{2,1,0:T(8,128)S(1)}, u32[]{:S(2)}, u32[]{:S(2)}) collective-permute-start(f32[2,7,256]{2,1,0:T(8,128)S(1)} %get-tuple-element.53), channel_id=1, source_target_pairs={{4,0},{8,4},{12,8},{5,1},{9,5},{13,9},{6,2},{10,6},{14,10},{7,3},{... | collective-permute-start | bytes 43016 | tf_op jit(solution)/shard_map/ppermute | solution.py:19
  13.7 1.2 %fusion.47 = (f32[256,270]{0,1:T(8,128)S(1)}, f32[256,270]{0,1:T(8,128)S(1)}, f32[256,270]{0,1:T(8,128)S(1)}, f32[256,270]{0,1:T(8,128)S(1)}, f32[256,270]{0,1:T...) fusion(s32[270]{0:T(512)S(1)} %iota_add_fusion), kind=kLoop, calls=%fused_computation.77 | loop fusion | flops 4423680 | bytes 8295480 | tf_op jit(solution)/shard_map/convert_element_type | solution.py:33
  16.7 1.2 %multiply_add_fusion.1 = f32[4,256,270]{1,2,0:T(8,128)S(1)} fusion(f32[256,270]{0,1:T(8,128)S(1)} %get-tuple-element.58, f32[4]{0:T(128)S(1)} %get-tuple-element.21, f32[256,270]{0,1:T(8,128)S(1)} %get-tuple-element.59, f32[4]{0:T(128)S(1)} %get-tuple-element.22, f32[256,270]{0,1:T(8,128)S(1)} %get-tuple-element.60, f32[4]{0:T(128)S(1)} %get-tuple-element.23, ...), kind=kLoop, calls=%fused_computation.19 | loop fusion | flops 8017920 | bytes 5253360 | tf_op jit(solution)/shard_map/add | solution.py:34
  17.9 1.2 %multiply_add_fusion = f32[4,256,270]{1,2,0:T(8,128)S(1)} fusion(f32[256,270]{0,1:T(8,128)S(1)} %get-tuple-element.72, f32[256,270]{0,1:T(8,128)S(1)} %get-tuple-element.73, f32[256,270]{0,1:T(8,128)S(1)} %get-tuple-element.74, f32[256,270]{0,1:T(8,128)S(1)} %get-tuple-element.75, f32[256,270]{0,1:T(8,128)S(1)} %get-tuple-element.76, ...), kind=kLoop, calls=%fused_computation.18 | loop fusion | flops 8017920 | bytes 5253360 | tf_op jit(solution)/shard_map/add | solution.py:34
  20.1 0.7 reduce_sum.19
  20.9 7.5 %all_gather.3 = f32[8,46,270]{2,1,0:T(8,128)S(1)} all-gather(f32[2,46,270]{2,1,0:T(8,128)S(1)} %select_maximum_fusion), channel_id=1, replica_groups=mesh['win'=2,'tile'=4,'view'=4] {'view'}, dimensions={0}, use_global_device_ids=true | all-gather | bytes 496800 | tf_op jit(solution)/shard_map/all_gather | solution.py:63
  28.4 0.5 convolution_bitcast_fusion.4
  29.0 0.5 convolution_bitcast_fusion.5
  29.5 0.5 convolution_bitcast_fusion.6
  30.0 0.5 convolution_bitcast_fusion.7
  30.5 0.8 fusion.8
  31.3 0.8 fusion.10
  32.1 0.8 fusion.12
  32.8 0.8 fusion.14
  34.7 0.5 fusion.1
  35.2 4.5 %collective-permute-start.2 = (f32[8,7,256]{2,0,1:T(8,128)S(1)}, f32[8,7,256]{2,0,1:T(8,128)S(1)}, u32[]{:S(2)}, u32[]{:S(2)}) collective-permute-start(f32[8,7,256]{2,0,1:T(8,128)S(1)} %get-tuple-element.50), channel_id=1, source_target_pairs={{0,4},{4,8},{8,12},{1,5},{5,9},{9,13},{2,6},{6,10},{10,14},{3,7},{... | collective-permute-start | bytes 172040 | tf_op jit(solution)/shard_map/ppermute | solution.py:17
  39.8 1.5 %collective-permute-start.3 = (f32[8,7,256]{2,0,1:T(8,128)S(1)}, f32[8,7,256]{2,0,1:T(8,128)S(1)}, u32[]{:S(2)}, u32[]{:S(2)}) collective-permute-start(f32[8,7,256]{2,0,1:T(8,128)S(1)} %get-tuple-element.51), channel_id=1, source_target_pairs={{4,0},{8,4},{12,8},{5,1},{9,5},{13,9},{6,2},{10,6},{14,10},{7,3},{... | collective-permute-start | bytes 172040 | tf_op jit(solution)/shard_map/ppermute | solution.py:19
  41.6 4.3 %collective-permute-done.3 = f32[8,7,256]{2,0,1:T(8,128)S(1)} collective-permute-done((f32[8,7,256]{2,0,1:T(8,128)S(1)}, f32[8,7,256]{2,0,1:T(8,128)S(1)}, u32[]{:S(2)}, u32[]{:S(2)}) %collective-permute-start.3) | collective-permute-done | bytes 57376 | tf_op jit(solution)/shard_map/ppermute | solution.py:19
  46.0 0.7 convolution_bitcast_fusion.3
  46.7 0.7 convolution_bitcast_fusion.2
  47.4 0.7 convolution_bitcast_fusion.1
  48.1 0.7 convolution_bitcast_fusion
  48.8 0.6 convolution_bitcast_fusion.12
  49.4 0.6 convolution_bitcast_fusion.11
  50.0 0.6 convolution_bitcast_fusion.10
  50.5 0.6 convolution_bitcast_fusion.9
  51.2 3.1 %fusion.2 = f32[8,32,256]{2,0,1:T(8,128)S(1)} fusion(f32[4,8,32,256]{3,2,1,0:T(8,128)S(1)} %pad_maximum_fusion, f32[]{:T(128)} %reduce_sum.19, f32[8,8]{1,0:T(8,128)S(1)} %fusion.245, f32[4]{0:T(128)S(1)} %get-tuple-element.6, f32[8,8]{1,0:T(8,128)S(1)} %get-tuple-element.144, f32[4]{0:T(128)S(1)} %get-tuple-element.7, f32[8,8]{1,0:T(8,128)S(1)} %get-tuple-element.143, ...), kind=kOutput, calls=%fused_computation.20 | convolution fusion | flops 25238784 | bytes 1314804 | tf_op jit(solution)/shard_map/rcz,rzay->cay/dot_general | solution.py:83
  54.3 0.8 copy.35
  55.1 19.6 %reduce-scatter.2.cloned.1.call-done = f32[2,32,256]{2,1,0:T(8,128)} async-done(((f32[8,32,256]{2,1,0:T(8,128)}), f32[2,32,256]{2,1,0:T(8,128)}) %reduce-scatter.2.cloned.1.call-update) | async-done | bytes 65552 | tf_op jit(solution)/shard_map/reduce_scatter | solution.py:82
  74.7 1.5 %multiply_bitcast_fusion = f32[2,1,32,256]{3,2,1,0:T(8,128)} fusion(f32[2,32,256]{2,1,0:T(8,128)} %reduce-scatter.2.cloned.1.call-done, f32[2,1,32,256]{3,2,1,0:T(8,128)S(1)} %copy-done), kind=kLoop, calls=%fused_computation.112 | loop fusion | flops 32768 | bytes 196608 | tf_op jit(solution)/shard_map/broadcast_in_dim | solution.py:88
  (47 shorter events, 3.9 us)
Async XLA Ops:
  6.5 68.1 %reduce-scatter.2.cloned.1.call-start = ((), (), s32[]{:S(2)}) async-start(), calls=%async_computation.1 | async-start | bytes 327680 | tf_op jit(solution)/shard_map/reduce_scatter | solution.py:82
  7.3 13.5 %collective-permute-start = (f32[2,7,256]{2,1,0:T(8,128)S(1)}, f32[2,7,256]{2,1,0:T(8,128)S(1)}, u32[]{:S(2)}, u32[]{:S(2)}) collective-permute-start(f32[2,7,256]{2,1,0:T(8,128)S(1)} %get-tuple-element.52), channel_id=1, source_target_pairs={{0,4},{4,8},{8,12},{1,5},{5,9},{9,13},{2,6},{6,10},{10,14},{3,7},{... | collective-permute-start | bytes 43016 | tf_op jit(solution)/shard_map/ppermute | solution.py:17
  12.2 8.6 %collective-permute-start.1 = (f32[2,7,256]{2,1,0:T(8,128)S(1)}, f32[2,7,256]{2,1,0:T(8,128)S(1)}, u32[]{:S(2)}, u32[]{:S(2)}) collective-permute-start(f32[2,7,256]{2,1,0:T(8,128)S(1)} %get-tuple-element.53), channel_id=1, source_target_pairs={{4,0},{8,4},{12,8},{5,1},{9,5},{13,9},{6,2},{10,6},{14,10},{7,3},{... | collective-permute-start | bytes 43016 | tf_op jit(solution)/shard_map/ppermute | solution.py:19
  13.7 1.2 %copy-start.1 = (f32[1,3,4,15]{3,2,1,0:T(4,128)S(1)}, f32[1,3,4,15]{3,2,1,0:T(4,128)}, u32[]{:S(2)}) copy-start(f32[1,3,4,15]{3,2,1,0:T(4,128)} %param.6) | copy-start | bytes 2164
  17.9 2.9 %copy-start = (f32[2,1,32,256]{3,2,1,0:T(8,128)S(1)}, f32[2,1,32,256]{3,2,1,0:T(8,128)}, u32[]{:S(2)}) copy-start(f32[2,1,32,256]{3,2,1,0:T(8,128)} %param.5) | copy-start | bytes 196612
  33.6 1.1 %copy-start.2 = (f32[1,8,1,32,256]{4,3,2,1,0:T(8,128)S(1)}, f32[1,8,1,32,256]{4,3,2,1,0:T(8,128)}, u32[]{:S(2)}) copy-start(f32[1,8,1,32,256]{4,3,2,1,0:T(8,128)} %param.4) | copy-start | bytes 786436
  35.2 6.4 %collective-permute-start.2 = (f32[8,7,256]{2,0,1:T(8,128)S(1)}, f32[8,7,256]{2,0,1:T(8,128)S(1)}, u32[]{:S(2)}, u32[]{:S(2)}) collective-permute-start(f32[8,7,256]{2,0,1:T(8,128)S(1)} %get-tuple-element.50), channel_id=1, source_target_pairs={{0,4},{4,8},{8,12},{1,5},{5,9},{9,13},{2,6},{6,10},{10,14},{3,7},{... | collective-permute-start | bytes 172040 | tf_op jit(solution)/shard_map/ppermute | solution.py:17
  39.8 6.1 %collective-permute-start.3 = (f32[8,7,256]{2,0,1:T(8,128)S(1)}, f32[8,7,256]{2,0,1:T(8,128)S(1)}, u32[]{:S(2)}, u32[]{:S(2)}) collective-permute-start(f32[8,7,256]{2,0,1:T(8,128)S(1)} %get-tuple-element.51), channel_id=1, source_target_pairs={{4,0},{8,4},{12,8},{5,1},{9,5},{13,9},{6,2},{10,6},{14,10},{7,3},{... | collective-permute-start | bytes 172040 | tf_op jit(solution)/shard_map/ppermute | solution.py:19
Sparse Core Ops, SparseCore 0:
  55.2 19.4 reduce-scatter.1
where the time goes:
time: 83.3 us; the launch traced here: 83 us
  waiting for transfers between devices  24.2 us (29%)
  matrix products  14.7 us (18%)
  between operations  14.5 us (17%)
  starting transfers between devices  12.3 us (15%)
  blocking collectives  7.53 us (9%)
  other arithmetic  6.94 us (8%)
  local copies, waits for them, and re-layouts  2.88 us (3%)
    reduce_scatter x1, waiting for transfers between devices, shards(): lax.psum_scatter(jnp.einsum('rcz,rzay->cay', adjoint_z, planes, precision...  19.6 us
    ppermute x2, starting transfers between devices, extended_2(): lax.ppermute(tail, axis, [(i, (i + 1) % count) for i in range(ends)])  9.49 us
    all_gather x1, blocking collectives, shards(): block_part = lax.all_gather(estimate_rim, 'view', axis=0, tiled=True)  7.53 us
    dot_general x8, matrix products, plane_pass(): return jnp.einsum('zay,cy->zac', section, matrix_y, precision=HIGHEST)  5.3 us
    dot_general x8, matrix products, plane_pass(): section = jnp.einsum('ab,zby->zay', matrix_x, volume, precision=HIGHEST)  4.81 us
    ppermute x2, waiting for transfers between devices, extended_2(): lax.ppermute(head, axis, [((i + 1) % count, i) for i in range(ends)])  4.27 us
    dot_general x1, matrix products, shards(): jnp.einsum('rcz,rzay->cay', adjoint_z, planes, precision=HIGHEST)  3.06 us
    add x5, other arithmetic, banded(): matrix = matrix + kernel[:, offset][:, None, None] * hit[None]  2.91 us
  transfers between devices with their start and end apart: 5, of which 3 were waited for; matrix products, arithmetic and copies ran while one was open for 8% of the time, Pallas kernels for 0%

commit v1 on v0

v1 whole, which is shorter than its diff:
```python
import functools

import jax
import jax.numpy as jnp
from jax import lax
from jax.experimental import pallas as pl
from jax.experimental.pallas import tpu as pltpu
from jax.sharding import PartitionSpec as P

F32 = jnp.float32
BF16 = jnp.bfloat16
HALO = 8
MESH = pl.DeviceIdType.MESH


def split(value):
    high = value.astype(BF16)
    return high, (value - high.astype(F32)).astype(BF16)


def dot(a, b):
    return jnp.dot(a, b, preferred_element_type=F32)


def dot3(a, b):
    return dot(a[0], b[0]) + (dot(a[0], b[1]) + dot(a[1], b[0]))


def rem_div(value, by):
    if by & (by - 1) == 0:
        return value & (by - 1), value >> (by.bit_length() - 1)
    return lax.rem(value, by), lax.div(value, by)


def iotas(shape):
    return lax.broadcasted_iota(jnp.int32, shape, 0), lax.broadcasted_iota(jnp.int32, shape, 1)


class Sizes:
    def __init__(self, slices, rows, columns, views, tiles, ranks, taps):
        self.slices, self.rows, self.columns = slices, rows, columns
        self.views, self.tiles, self.ranks, self.taps = views, tiles, ranks, taps
        self.depth = slices * views
        self.radius = taps // 2
        self.zb = 8 if self.depth % 8 == 0 else self.depth
        self.blocks = self.depth // self.zb
        reach = (self.radius + self.zb - 1) // self.zb
        self.diffs = [d for d in range(-reach, reach + 1) if abs(d) < self.blocks]
        assert self.radius <= HALO and rows >= HALO


def kernel(n, meas_hbm, est_hbm, taps_ref, back_ref, out_ref,
           meas, est, rim, quo, qrim, corr, parts,
           y_mat, own_mat, rim_mat,
           local_sem, g_send, g_recv, r_send, r_recv, f_send, f_recv, q_send, q_recv, s_send, s_recv):
    v = lax.axis_index("view")
    t = lax.axis_index("tile")
    not_first, not_last = t > 0, t < n.tiles - 1
    barrier = pltpu.get_barrier_semaphore()
    peers = [lax.rem(v + k, n.views) for k in range(1, n.views)]
    sides = ((not_first, t - 1), (not_last, t + 1))

    for p in peers:
        pl.semaphore_signal(barrier, inc=1, device_id={"view": p}, device_id_type=MESH)
    for there, other in sides:
        @pl.when(there)
        def _():
            pl.semaphore_signal(barrier, inc=1, device_id={"tile": other}, device_id_type=MESH)

    mine = pl.ds(v * n.slices, n.slices)
    load_meas = pltpu.make_async_copy(meas_hbm, meas, local_sem.at[0])
    load_est = pltpu.make_async_copy(est_hbm, est.at[mine], local_sem.at[1])
    load_meas.start()
    load_est.start()

    def tap(dim, r, k):
        return taps_ref[(dim * n.ranks + r) * n.taps + k]

    def banded(index, dim, r, direction):
        total = jnp.zeros(index.shape, F32)
        for k in range(n.taps):
            kk = k if direction > 0 else n.taps - 1 - k
            total = jnp.where(index == k, tap(dim, r, kk), total)
        return total

    def build_y(side, direction):
        s, l = iotas((8, n.columns))
        plain = s - l + n.radius
        wrapped = jnp.where(plain < 0, plain + n.columns, plain)
        count = n.columns // 8
        for r in range(n.ranks):
            base = banded(wrapped, 2, r, direction)
            pieces = [banded(plain, 2, r, direction)]
            for i in range(1, count):
                piece = pltpu.roll(base, 8 * i, 1)
                if i == count - 1:
                    piece = jnp.where(l >= n.columns // 2, piece, 0.0)
                pieces.append(piece)
            high, low = split(jnp.concatenate(pieces, axis=0))
            cols = slice(r * n.columns, (r + 1) * n.columns)
            y_mat[side, 0, :, cols] = high
            y_mat[side, 1, :, cols] = low

    def build_zx(side, direction, scale):
        for mat, width in ((own_mat, n.rows), (rim_mat, 2 * HALO)):
            lanes = n.zb * width
            x, l = iotas((n.rows, lanes))
            j = rem_div(l, width)[0]
            if width == n.rows and mat is own_mat:
                position = j
            else:
                position = jnp.where(j < HALO, j - HALO, j - HALO + n.rows)
            x_index = position - x + n.radius
            c, lz = iotas((n.zb, lanes))
            z = rem_div(lz, width)[1]
            for r in range(n.ranks):
                x_band = banded(x_index, 1, r, direction)
                for di, d in enumerate(n.diffs):
                    z_band = banded(z + (d * n.zb + n.radius) - c, 0, r, direction)
                    if scale is not None:
                        z_band = z_band * scale
                    whole = jnp.concatenate(
                        [x_band * z_band[i:i + 1, :] for i in range(n.zb)], axis=0)
                    high, low = split(whole)
                    cols = slice(r * lanes, (r + 1) * lanes)
                    mat[side, di, 0, :, cols] = high
                    mat[side, di, 1, :, cols] = low

    build_y(0, 1)

    pl.semaphore_wait(barrier, n.views - 1 + not_first.astype(jnp.int32) + not_last.astype(jnp.int32))

    def remote(src, dst, send, recv, where):
        return pltpu.make_async_remote_copy(
            src_ref=src, dst_ref=dst, send_sem=send, recv_sem=recv,
            device_id=where, device_id_type=MESH)

    halves = (slice(HALO, 2 * HALO), slice(0, HALO))
    edges = (slice(0, HALO), slice(n.rows - HALO, n.rows))
    rim_copies = [
        remote(est_hbm.at[:, edges[i], :], rim.at[mine, halves[i], :],
               r_send.at[i], r_recv.at[i], {"tile": sides[i][1]})
        for i in range(2)]
    for (there, _o), copy in zip(sides, rim_copies):
        pl.when(there)(copy.start)
    gathers = [
        remote(est_hbm, est.at[mine], g_send.at[k], g_recv.at[k], {"view": p})
        for k, p in enumerate(peers)]
    for copy in gathers:
        copy.start()

    for i, (there, _o) in enumerate(sides):
        @pl.when(jnp.logical_not(there))
        def _():
            zeros = jnp.zeros((n.depth, HALO, n.columns), F32)
            rim[:, slice(i * HALO, (i + 1) * HALO), :] = zeros
            qrim[:, slice(i * HALO, (i + 1) * HALO), :] = zeros

    build_zx(0, 1, None)

    forwards = []
    for i, (there, _o) in enumerate(sides):
        here = rim.at[mine, slice(i * HALO, (i + 1) * HALO), :]
        copies = [remote(here, here, f_send.at[i, k], f_recv.at[i, k], {"view": p})
                  for k, p in enumerate(peers)]
        forwards.append(copies)

        @pl.when(there)
        def _():
            rim_copies[1 - i].wait_recv()
            for copy in copies:
                copy.start()

    norm = 0.0
    for r in range(n.ranks):
        term = 1.0
        for dim in range(3):
            term = term * functools.reduce(lambda a, b: a + b, [tap(dim, r, k) for k in range(n.taps)])
        norm = norm + term
    inverse = 1.0 / jnp.full((1, 1), norm, F32)
    build_y(1, -1)
    build_zx(1, -1, inverse)

    def pass_y(side, rows):
        return split(dot3(split(rows), (y_mat[side, 0], y_mat[side, 1])))

    def sections(side, ref, width):
        return [pass_y(side, ref[b * n.zb:(b + 1) * n.zb].reshape(n.zb * width, n.columns))
                for b in range(n.blocks)]

    def pass_zx(side, mat, planes, bo):
        total = None
        for di, d in enumerate(n.diffs):
            if not 0 <= bo + d < n.blocks:
                continue
            plane = planes[bo + d]
            lanes = plane[0].shape[0]
            for r in range(n.ranks):
                left = tuple(mat[side, di, h, :, r * lanes:(r + 1) * lanes] for h in range(2))
                right = tuple(part[:, r * n.columns:(r + 1) * n.columns] for part in plane)
                term = dot3(left, right)
                total = term if total is None else total + term
        return total

    load_est.wait()
    for copy in gathers:
        copy.wait_recv()
    planes = sections(0, est, n.rows)
    inner = [pass_zx(0, own_mat, planes, b) for b in range(n.blocks)]
    for (there, _o), copies in zip(sides, forwards):
        @pl.when(there)
        def _():
            for copy in copies:
                copy.wait_recv()
    load_meas.wait()
    outer = sections(0, rim, 2 * HALO)
    for b in range(n.blocks):
        predicted = inner[b] + pass_zx(0, rim_mat, outer, b) + back_ref[0]
        zs = slice(b * n.zb, (b + 1) * n.zb)
        quo[zs] = meas[zs] / predicted.reshape(n.zb, n.rows, n.columns)

    q_copies = [
        remote(quo.at[:, edges[i], :], qrim.at[:, halves[i], :],
               q_send.at[i], q_recv.at[i], {"tile": sides[i][1]})
        for i in range(2)]
    for (there, _o), copy in zip(sides, q_copies):
        pl.when(there)(copy.start)
    planes = sections(1, quo, n.rows)
    inner = [pass_zx(1, own_mat, planes, b) for b in range(n.blocks)]
    for i, (there, _o) in enumerate(sides):
        pl.when(there)(q_copies[1 - i].wait_recv)
    outer = sections(1, qrim, 2 * HALO)
    for b in range(n.blocks):
        zs = slice(b * n.zb, (b + 1) * n.zb)
        corr[zs] = (inner[b] + pass_zx(1, rim_mat, outer, b)).reshape(n.zb, n.rows, n.columns)

    scatters = [
        remote(corr.at[pl.ds(p * n.slices, n.slices)], parts.at[k], s_send.at[k], s_recv.at[k], {"view": p})
        for k, p in enumerate(peers)]
    for copy in scatters:
        copy.start()
    total = corr[mine]
    for k, copy in enumerate(scatters):
        copy.wait_recv()
        total = total + parts[k]
    out_ref[...] = est[mine] * total * (1.0 / n.views)

    for (there, _o), copies in zip(sides, zip(rim_copies, q_copies)):
        @pl.when(there)
        def _():
            for copy in copies:
                copy.wait_send()
    for i, (there, _o) in enumerate(sides):
        @pl.when(there)
        def _():
            for copy in forwards[i]:
                copy.wait_send()
    for copy in gathers + scatters:
        copy.wait_send()


def shards(sizes, measured, estimate, psf_taps, background):
    n = sizes
    plane = (n.depth, n.rows, n.columns)
    rims = (n.depth, 2 * HALO, n.columns)
    own = n.zb * n.rows
    out = pl.pallas_call(
        functools.partial(kernel, n),
        out_shape=jax.ShapeDtypeStruct((n.slices, n.rows, n.columns), F32),
        in_specs=[
            pl.BlockSpec(memory_space=pl.ANY),
            pl.BlockSpec(memory_space=pl.ANY),
            pl.BlockSpec(memory_space=pltpu.SMEM),
            pl.BlockSpec(memory_space=pltpu.SMEM),
        ],
        out_specs=pl.BlockSpec(memory_space=pltpu.VMEM),
        scratch_shapes=[
            pltpu.VMEM(plane, F32),
            pltpu.VMEM(plane, F32),
            pltpu.VMEM(rims, F32),
            pltpu.VMEM(plane, F32),
            pltpu.VMEM(rims, F32),
            pltpu.VMEM(plane, F32),
            pltpu.VMEM((n.views - 1, n.slices, n.rows, n.columns), F32),
            pltpu.VMEM((2, 2, n.columns, n.ranks * n.columns), BF16),
            pltpu.VMEM((2, len(n.diffs), 2, own, n.ranks * own), BF16),
            pltpu.VMEM((2, len(n.diffs), 2, own, n.ranks * n.zb * 2 * HALO), BF16),
            pltpu.SemaphoreType.DMA((2,)),
            pltpu.SemaphoreType.DMA((n.views - 1,)),
            pltpu.SemaphoreType.DMA((n.views - 1,)),
            pltpu.SemaphoreType.DMA((2,)),
            pltpu.SemaphoreType.DMA((2,)),
            pltpu.SemaphoreType.DMA((2, n.views - 1)),
            pltpu.SemaphoreType.DMA((2, n.views - 1)),
            pltpu.SemaphoreType.DMA((2,)),
            pltpu.SemaphoreType.DMA((2,)),
            pltpu.SemaphoreType.DMA((n.views - 1,)),
            pltpu.SemaphoreType.DMA((n.views - 1,)),
        ],
        compiler_params=pltpu.CompilerParams(
            collective_id=0, has_side_effects=True, vmem_limit_bytes=56 * 1024 * 1024),
    )(measured[0, :, 0], estimate[:, 0], psf_taps.reshape(-1), background)
    return out[:, None]


def solution(mesh):
    def body(measured, estimate, psf_taps, background):
        sizes = Sizes(estimate.shape[0], estimate.shape[2], estimate.shape[3],
                      mesh.shape["view"], mesh.shape["tile"], psf_taps.shape[2], psf_taps.shape[3])
        return shards(sizes, measured, estimate, psf_taps, background)

    return jax.shard_map(
        body,
        mesh=mesh,
        in_specs=(
            P("view", None, ("win", "tile"), None, None),
            P("view", ("win", "tile"), None, None),
            P("view", None, None, None),
            P("view"),
        ),
        out_specs=P("view", ("win", "tile"), None, None),
        check_vma=False,
    )
```

time: 83.3 us -> 26.1 us (0.31)
  waiting for transfers between devices: 24.2 us -> 0 us
  Pallas kernels: 0 us -> 22.4 us
  matrix products: 14.7 us -> 0 us
  between operations: 14.5 us -> 0.66 us
  starting transfers between devices: 12.3 us -> 0 us
  blocking collectives: 7.53 us -> 0 us
  other arithmetic: 6.94 us -> 0 us
    pallas_call x0 -> x1, Pallas kernels: none -> 22.4 us  [shards(): pl.pallas_call(functools.partial(kernel, n), out_shape=jax.ShapeDtypeStru...]
    reduce_scatter x1 -> x0, waiting for transfers between devices: 19.6 us -> none  [shards(): lax.psum_scatter(jnp.einsum('rcz,rzay->cay', adjoint_z, planes, precision...]
    dot_general x21 -> x0, matrix products: 14.7 us -> none  [the longest x8 5.3 us: plane_pass(): return jnp.einsum('zay,cy->zac', section, matrix_y, precision=HIGHEST)]
    ppermute x4 -> x0, starting transfers between devices: 12.3 us -> none  [the longest x2 9.49 us: extended_2(): lax.ppermute(tail, axis, [(i, (i + 1) % count) for i in range(ends)])]
    all_gather x1 -> x0, blocking collectives: 7.53 us -> none  [shards(): block_part = lax.all_gather(estimate_rim, 'view', axis=0, tiled=True)]
    ppermute x4 -> x0, waiting for transfers between devices: 4.58 us -> none  [the longest x2 4.27 us: extended_2(): lax.ppermute(head, axis, [((i + 1) % count, i) for i in range(ends)])]
    add x5 -> x0, other arithmetic: 2.91 us -> none  [banded(): matrix = matrix + kernel[:, offset][:, None, None] * hit[None]]
    slice x5 -> x0, local copies, waits for them, and re-layouts: 1.95 us -> none  [the longest x3 1.21 us: banded(): matrix = matrix + kernel[:, offset][:, None, None] * hit[None]]
  transfers between devices with their start and end apart: 5 -> 0, of which waited for: 3 -> 0; matrix products, arithmetic and copies ran while one was open for 8% -> 0% of each run, Pallas kernels for 0% -> 0%
where the time goes in v1:
time: 26.1 us; the launch traced here: 25.8 us
  Pallas kernels  22.4 us (86%)
  local copies, waits for them, and re-layouts  2.82 us (11%)
  between operations  0.66 us (3%)
    pallas_call x1, Pallas kernels, shards(): pl.pallas_call(functools.partial(kernel, n), out_shape=jax.ShapeDtypeStru...  22.4 us
    unnamed x1, local copies, waits for them, and re-layouts  1.47 us
    reshape x1, local copies, waits for them, and re-layouts, shards(): psf_taps.reshape(-1)  1.35 us

profile of v1, /device:TPU:0, one launch (start us, length us, event | category | flops | bytes accessed | tf_op | source)
XLA Modules:
  0.0 25.8 jit_solution(4332107978541477073)
XLA Ops:
  0.7 1.3 %reshape.3.taps_ref = f32[180]{0:T(256)} reshape(f32[1,3,4,15]{3,2,1,0:T(4,128)} %param.6) | data formatting | bytes 1440 | tf_op jit(solution)/shard_map/reshape | solution.py:302
  2.0 22.4 %shard_map.46 = f32[2,32,256]{2,1,0:T(8,128)} custom-call(f32[8,32,256]{2,1,0:T(8,128)} %bitcast.5, f32[2,32,256]{2,1,0:T(8,128)} %bitcast.7, f32[180]{0:T(256)} %reshape.3.taps_ref, f32[1]{0:T(128)S(6)} %copy.7.back_ref), custom_call_target="tpu_custom_call" | custom-call | tf_op jit(solution)/shard_map/pallas_call | solution.py:267
  24.4 1.5 %copy.8 = f32[2,1,32,256]{3,2,1,0:T(8,128)} copy(f32[2,1,32,256]{3,2,1,0:T(8,128)} %bitcast.6) | data formatting | bytes 131072

commit v2 on v1

v2 whole, which is shorter than its diff:
```python
import functools

import jax
import jax.numpy as jnp
from jax import lax
from jax.experimental import pallas as pl
from jax.experimental.pallas import tpu as pltpu
from jax.sharding import PartitionSpec as P

F32 = jnp.float32
BF16 = jnp.bfloat16
HALO = 8
MESH = pl.DeviceIdType.MESH


def split(value):
    high = value.astype(BF16)
    return high, (value - high.astype(F32)).astype(BF16)


def dot(a, b):
    return jnp.dot(a, b, preferred_element_type=F32)


def rem_div(value, by):
    if by & (by - 1) == 0:
        return value & (by - 1), value >> (by.bit_length() - 1)
    return lax.rem(value, by), lax.div(value, by)


def iotas(shape):
    return lax.broadcasted_iota(jnp.int32, shape, 0), lax.broadcasted_iota(jnp.int32, shape, 1)


class Sizes:
    def __init__(self, slices, rows, columns, views, tiles, ranks, taps):
        self.slices, self.rows, self.columns = slices, rows, columns
        self.views, self.tiles, self.ranks, self.taps = views, tiles, ranks, taps
        self.depth = slices * views
        self.radius = taps // 2
        self.zb = 8 if self.depth % 8 == 0 else self.depth
        self.blocks = self.depth // self.zb
        reach = (self.radius + self.zb - 1) // self.zb
        self.diffs = [d for d in range(-reach, reach + 1) if abs(d) < self.blocks]
        assert self.radius <= HALO and rows >= 2 * HALO


def kernel(n, meas_hbm, est_hbm, taps_ref, back_ref, out_ref,
           meas, mrim, est, rim, quo, qrim, corr, parts,
           y_mat, fwd_own, fwd_rim, adj,
           local_sem, g_send, g_recv, r_send, r_recv, m_send, m_recv, s_send, s_recv):
    v = lax.axis_index("view")
    t = lax.axis_index("tile")
    not_first, not_last = t > 0, t < n.tiles - 1
    barrier = pltpu.get_barrier_semaphore()
    views = [lax.rem(v + k, n.views) for k in range(n.views)]
    peers = views[1:]
    sides = ((not_first, t - 1), (not_last, t + 1))

    for there, other in sides:
        @pl.when(there)
        def _():
            for p in views:
                pl.semaphore_signal(
                    barrier, inc=1, device_id={"tile": other, "view": p}, device_id_type=MESH)
    for p in peers:
        pl.semaphore_signal(barrier, inc=1, device_id={"view": p}, device_id_type=MESH)

    mine = pl.ds(v * n.slices, n.slices)
    load_meas = pltpu.make_async_copy(meas_hbm, meas, local_sem.at[0])
    load_est = pltpu.make_async_copy(est_hbm, est.at[mine], local_sem.at[1])
    load_meas.start()
    load_est.start()

    def tap(dim, r, k):
        return taps_ref[0, dim, r, k]

    def banded(index, dim, r, direction):
        total = jnp.zeros(index.shape, F32)
        for k in range(n.taps):
            kk = k if direction > 0 else n.taps - 1 - k
            total = jnp.where(index == k, tap(dim, r, kk), total)
        return total

    def build_y(side, direction):
        s, l = iotas((8, n.columns))
        plain = s - l + n.radius
        wrapped = jnp.where(plain < 0, plain + n.columns, plain)
        count = n.columns // 8
        for r in range(n.ranks):
            base = banded(wrapped, 2, r, direction)
            pieces = [banded(plain, 2, r, direction)]
            for i in range(1, count):
                piece = pltpu.roll(base, 8 * i, 1)
                if i == count - 1:
                    piece = jnp.where(l >= n.columns // 2, piece, 0.0)
                pieces.append(piece)
            high, low = split(jnp.concatenate(pieces, axis=0))
            for part, value in enumerate((high, low)):
                begin = (part * n.ranks + r) * n.columns
                y_mat[side, begin:begin + n.columns, :] = value

    def position(index, halo):
        if halo == 0:
            return index
        return jnp.where(index < halo, index - halo, index - halo + n.rows)

    def build_zx(mat, first, stride, out_halo, in_halo, direction, scale):
        width = 2 * in_halo if in_halo else n.rows
        lanes = n.zb * width
        c, lz = iotas((n.zb, lanes))
        z = rem_div(lz, width)[1]
        for r in range(n.ranks):
            x_bands = []
            for halo in (0, out_halo) if out_halo else (0,):
                x, l = iotas((2 * halo if halo else n.rows, lanes))
                index = position(rem_div(l, width)[0], in_halo) - position(x, halo) + n.radius
                x_bands.append(banded(index, 1, r, direction))
            for di, d in enumerate(n.diffs):
                z_band = banded(z + (d * n.zb + n.radius) - c, 0, r, direction)
                if scale is not None:
                    z_band = z_band * scale
                whole = jnp.concatenate(
                    [x_band * z_band[i:i + 1, :] for x_band in x_bands for i in range(n.zb)], axis=0)
                high, low = split(whole)
                rows = slice(r * whole.shape[0], (r + 1) * whole.shape[0])
                mat[di, rows, first:first + lanes] = high
                mat[di, rows, stride + first:stride + first + lanes] = low

    build_y(0, 1)

    arrivals = n.views * (not_first.astype(jnp.int32) + not_last.astype(jnp.int32)) + n.views - 1
    pl.semaphore_wait(barrier, arrivals)

    def remote(src, dst, send, recv, where):
        return pltpu.make_async_remote_copy(
            src_ref=src, dst_ref=dst, send_sem=send, recv_sem=recv,
            device_id=where, device_id_type=MESH)

    def edge(side, halo):
        return slice(0, halo) if side == 0 else slice(n.rows - halo, n.rows)

    def half(side, halo):
        return slice(0, halo) if side == 0 else slice(halo, 2 * halo)

    rim_copies = [
        [remote(est_hbm.at[:, edge(i, 2 * HALO), :], rim.at[mine, half(1 - i, 2 * HALO), :],
                r_send.at[i, k], r_recv.at[i, k], {"tile": sides[i][1], "view": p})
         for k, p in enumerate(views)]
        for i in range(2)]
    m_copies = [
        remote(meas_hbm.at[:, edge(i, HALO), :], mrim.at[:, half(1 - i, HALO), :],
               m_send.at[i], m_recv.at[i], {"tile": sides[i][1]})
        for i in range(2)]
    gathers = [
        remote(est_hbm, est.at[mine], g_send.at[k], g_recv.at[k], {"view": p})
        for k, p in enumerate(peers)]
    for copy in gathers:
        copy.start()
    for i, (there, _o) in enumerate(sides):
        @pl.when(there)
        def _():
            for copy in rim_copies[i]:
                copy.start()
    for i, (there, _o) in enumerate(sides):
        pl.when(there)(m_copies[i].start)

        @pl.when(jnp.logical_not(there))
        def _():
            rim[:, half(i, 2 * HALO), :] = jnp.zeros((n.depth, 2 * HALO, n.columns), F32)
            mrim[:, half(i, HALO), :] = jnp.zeros((n.depth, HALO, n.columns), F32)

    norm = 0.0
    for r in range(n.ranks):
        term = 1.0
        for dim in range(3):
            term = term * functools.reduce(lambda a, b: a + b, [tap(dim, r, k) for k in range(n.taps)])
        norm = norm + term
    inverse = 1.0 / jnp.full((1, 1), norm, F32)
    k_own, k_rim = (n.zb * width for width in (n.rows, 4 * HALO))
    k_adj = k_own + k_rim // 2
    build_zx(fwd_own, 0, k_own, HALO, 0, 1, None)
    build_zx(fwd_rim, 0, k_rim, HALO, 2 * HALO, 1, None)
    build_y(1, -1)
    build_zx(adj, 0, k_adj, 0, 0, -1, inverse)
    build_zx(adj, k_own, k_adj, 0, HALO, -1, inverse)

    def blocks_of(ref, width):
        return [split(ref[b * n.zb:(b + 1) * n.zb].reshape(n.zb * width, n.columns))
                for b in range(n.blocks)]

    def pass_zx(mat, sources, bo):
        total = None
        for di, d in enumerate(n.diffs):
            if not 0 <= bo + d < n.blocks:
                continue
            high, low = ([blocks[bo + d][h] for blocks in sources] for h in range(2))
            term = dot(mat[di], jnp.concatenate(high + high, axis=0))
            term = term + dot(mat[di, :, :mat.shape[2] // 2], jnp.concatenate(low, axis=0))
            total = term if total is None else total + term
        return total

    def pass_y(side, terms):
        rows = terms.shape[0] // n.ranks
        high, low = ([part[r * rows:(r + 1) * rows] for r in range(n.ranks)] for part in split(terms))
        return (dot(jnp.concatenate(high + high, axis=1), y_mat[side])
                + dot(jnp.concatenate(low, axis=1), y_mat[side, :n.ranks * n.columns]))

    load_est.wait()
    for copy in gathers:
        copy.wait_recv()
    planes = blocks_of(est, n.rows)
    inner = [pass_zx(fwd_own, [planes], b) for b in range(n.blocks)]
    for i, (there, _o) in enumerate(sides):
        @pl.when(there)
        def _():
            for copy in rim_copies[1 - i]:
                copy.wait_recv()
            m_copies[1 - i].wait_recv()
    load_meas.wait()
    outer = blocks_of(rim, 4 * HALO)
    own = n.zb * n.rows
    for b in range(n.blocks):
        predicted = pass_y(0, inner[b] + pass_zx(fwd_rim, [outer], b)) + back_ref[...]
        zs = slice(b * n.zb, (b + 1) * n.zb)
        quo[zs] = meas[zs] / predicted[:own].reshape(n.zb, n.rows, n.columns)
        qrim[zs] = mrim[zs] / predicted[own:].reshape(n.zb, 2 * HALO, n.columns)

    planes = blocks_of(quo, n.rows)
    outer = blocks_of(qrim, 2 * HALO)
    for b in range(n.blocks):
        zs = slice(b * n.zb, (b + 1) * n.zb)
        corr[zs] = pass_y(1, pass_zx(adj, [planes, outer], b)).reshape(n.zb, n.rows, n.columns)

    scatters = [
        remote(corr.at[pl.ds(p * n.slices, n.slices)], parts.at[k], s_send.at[k], s_recv.at[k], {"view": p})
        for k, p in enumerate(peers)]
    for copy in scatters:
        copy.start()
    total = corr[mine]
    for k, copy in enumerate(scatters):
        copy.wait_recv()
        total = total + parts[k]
    out_ref[...] = est[mine] * total * (1.0 / n.views)

    for i, (there, _o) in enumerate(sides):
        @pl.when(there)
        def _():
            for copy in rim_copies[i]:
                copy.wait_send()
            m_copies[i].wait_send()
    for copy in gathers + scatters:
        copy.wait_send()


def shards(sizes, measured, estimate, psf_taps, background):
    n = sizes
    plane = (n.depth, n.rows, n.columns)
    rims = (n.depth, 2 * HALO, n.columns)
    own, outs, diffs = n.zb * n.rows, n.zb * (n.rows + 2 * HALO), len(n.diffs)
    dma = pltpu.SemaphoreType.DMA
    out = pl.pallas_call(
        functools.partial(kernel, n),
        out_shape=jax.ShapeDtypeStruct((n.slices, n.rows, n.columns), F32),
        in_specs=[
            pl.BlockSpec(memory_space=pl.ANY),
            pl.BlockSpec(memory_space=pl.ANY),
            pl.BlockSpec(memory_space=pltpu.SMEM),
            pl.BlockSpec(memory_space=pltpu.VMEM),
        ],
        out_specs=pl.BlockSpec(memory_space=pltpu.VMEM),
        scratch_shapes=[
            pltpu.VMEM(plane, F32),
            pltpu.VMEM(rims, F32),
            pltpu.VMEM(plane, F32),
            pltpu.VMEM((n.depth, 4 * HALO, n.columns), F32),
            pltpu.VMEM(plane, F32),
            pltpu.VMEM(rims, F32),
            pltpu.VMEM(plane, F32),
            pltpu.VMEM((n.views - 1, n.slices, n.rows, n.columns), F32),
            pltpu.VMEM((2, 2 * n.ranks * n.columns, n.columns), BF16),
            pltpu.VMEM((diffs, n.ranks * outs, 2 * own), BF16),
            pltpu.VMEM((diffs, n.ranks * outs, 2 * n.zb * 4 * HALO), BF16),
            pltpu.VMEM((diffs, n.ranks * own, 2 * n.zb * (n.rows + 2 * HALO)), BF16),
            dma((2,)),
            dma((n.views - 1,)),
            dma((n.views - 1,)),
            dma((2, n.views)),
            dma((2, n.views)),
            dma((2,)),
            dma((2,)),
            dma((n.views - 1,)),
            dma((n.views - 1,)),
        ],
        compiler_params=pltpu.CompilerParams(
            collective_id=0, has_side_effects=True, vmem_limit_bytes=56 * 1024 * 1024),
    )(measured[0, :, 0], estimate[:, 0], psf_taps, background.reshape(1, 1))
    return out[:, None]


def solution(mesh):
    def body(measured, estimate, psf_taps, background):
        sizes = Sizes(estimate.shape[0], estimate.shape[2], estimate.shape[3],
                      mesh.shape["view"], mesh.shape["tile"], psf_taps.shape[2], psf_taps.shape[3])
        return shards(sizes, measured, estimate, psf_taps, background)

    return jax.shard_map(
        body,
        mesh=mesh,
        in_specs=(
            P("view", None, ("win", "tile"), None, None),
            P("view", ("win", "tile"), None, None),
            P("view", None, None, None),
            P("view"),
        ),
        out_specs=P("view", ("win", "tile"), None, None),
        check_vma=False,
    )
```

time: 26.1 us -> 24.3 us (0.931)
  the two profiles are of different devices: /device:TPU:0 before, /device:TPU:13 now
where the time goes in v2:
time: 24.3 us; the launch traced here: 24.1 us
  Pallas kernels  21.9 us (90%)
  local copies, waits for them, and re-layouts  1.47 us (6%)
  between operations  0.66 us (3%)
    pallas_call x1, Pallas kernels, shards(): pl.pallas_call(functools.partial(kernel, n), out_shape=jax.ShapeDtypeStru...  21.9 us
    unnamed x1, local copies, waits for them, and re-layouts  1.47 us

profile of v2, /device:TPU:13, one launch (start us, length us, event | category | flops | bytes accessed | tf_op | source)
XLA Modules:
  0.0 24.1 jit_solution(18444960354414957882)
XLA Ops:
  0.7 21.9 %shard_map.46 = f32[2,32,256]{2,1,0:T(8,128)} custom-call(f32[8,32,256]{2,1,0:T(8,128)} %bitcast.8, f32[2,32,256]{2,1,0:T(8,128)} %bitcast.9, f32[1,3,4,15]{3,2,1,0:T(4,128)} %taps_ref.1, f32[1,1]{1,0:T(1,128)} %bitcast.6.back_ref), custom_call_target="tpu_custom_call" | custom-call | tf_op jit(solution)/shard_map/pallas_call | solution.py:262
  22.6 1.5 %copy.8 = f32[2,1,32,256]{3,2,1,0:T(8,128)} copy(f32[2,1,32,256]{3,2,1,0:T(8,128)} %bitcast.7) | data formatting | bytes 131072

commit v3 on v2

--- a/solution.py
+++ b/solution.py
@@ -46,7 +46,7 @@
 
 
 def kernel(n, meas_hbm, est_hbm, taps_ref, back_ref, out_ref,
-           meas, mrim, est, rim, quo, qrim, corr, parts,
+           meas, mrim, est, rim, quo, qrim, corr,
            y_mat, fwd_own, fwd_rim, adj,
            local_sem, g_send, g_recv, r_send, r_recv, m_send, m_recv, s_send, s_recv):
     v = lax.axis_index("view")
@@ -233,16 +233,15 @@
         corr[zs] = pass_y(1, pass_zx(adj, [planes, outer], b)).reshape(n.zb, n.rows, n.columns)
 
     scatters = [
-        remote(corr.at[pl.ds(p * n.slices, n.slices)], parts.at[k], s_send.at[k], s_recv.at[k], {"view": p})
+        remote(corr.at[pl.ds(p * n.slices, n.slices)], out_ref.at[k], s_send.at[k], s_recv.at[k], {"view": p})
         for k, p in enumerate(peers)]
     for copy in scatters:
         copy.start()
-    total = corr[mine]
-    for k, copy in enumerate(scatters):
+    keep = pltpu.make_async_copy(corr.at[mine], out_ref.at[n.views - 1], local_sem.at[2])
+    keep.start()
+    for copy in scatters:
         copy.wait_recv()
-        total = total + parts[k]
-    out_ref[...] = est[mine] * total * (1.0 / n.views)
-
+    keep.wait()
     for i, (there, _o) in enumerate(sides):
         @pl.when(there)
         def _():
@@ -261,14 +260,14 @@
     dma = pltpu.SemaphoreType.DMA
     out = pl.pallas_call(
         functools.partial(kernel, n),
-        out_shape=jax.ShapeDtypeStruct((n.slices, n.rows, n.columns), F32),
+        out_shape=jax.ShapeDtypeStruct((n.views, n.slices, n.rows, n.columns), F32),
         in_specs=[
             pl.BlockSpec(memory_space=pl.ANY),
             pl.BlockSpec(memory_space=pl.ANY),
             pl.BlockSpec(memory_space=pltpu.SMEM),
             pl.BlockSpec(memory_space=pltpu.VMEM),
         ],
-        out_specs=pl.BlockSpec(memory_space=pltpu.VMEM),
+        out_specs=pl.BlockSpec(memory_space=pl.ANY),
         scratch_shapes=[
             pltpu.VMEM(plane, F32),
             pltpu.VMEM(rims, F32),
@@ -277,12 +276,11 @@
             pltpu.VMEM(plane, F32),
             pltpu.VMEM(rims, F32),
             pltpu.VMEM(plane, F32),
-            pltpu.VMEM((n.views - 1, n.slices, n.rows, n.columns), F32),
             pltpu.VMEM((2, 2 * n.ranks * n.columns, n.columns), BF16),
             pltpu.VMEM((diffs, n.ranks * outs, 2 * own), BF16),
             pltpu.VMEM((diffs, n.ranks * outs, 2 * n.zb * 4 * HALO), BF16),
             pltpu.VMEM((diffs, n.ranks * own, 2 * n.zb * (n.rows + 2 * HALO)), BF16),
-            dma((2,)),
+            dma((3,)),
             dma((n.views - 1,)),
             dma((n.views - 1,)),
             dma((2, n.views)),
@@ -295,7 +293,7 @@
         compiler_params=pltpu.CompilerParams(
             collective_id=0, has_side_effects=True, vmem_limit_bytes=56 * 1024 * 1024),
     )(measured[0, :, 0], estimate[:, 0], psf_taps, background.reshape(1, 1))
-    return out[:, None]
+    return estimate * jnp.sum(out, axis=0)[:, None] * (1.0 / n.views)
 
 
 def solution(mesh):

time: 24.3 us -> 23.9 us (0.984)
  the two profiles are of different devices: /device:TPU:13 before, /device:TPU:17 now
where the time goes in v3:
time: 23.9 us; the launch traced here: 23.8 us
  Pallas kernels  21.4 us (90%)
  other arithmetic  1.64 us (7%)
  between operations  0.68 us (3%)
    pallas_call x1, Pallas kernels, shards(): pl.pallas_call(functools.partial(kernel, n), out_shape=jax.ShapeDtypeStru...  21.4 us
    reduce_sum x1, other arithmetic, shards(): return estimate * jnp.sum(out, axis=0)[:, None] * (1.0 / n.views)  1 us
    mul x1, other arithmetic, shards(): return estimate * jnp.sum(out, axis=0)[:, None] * (1.0 / n.views)  0.64 us

profile of v3, /device:TPU:17, one launch (start us, length us, event | category | flops | bytes accessed | tf_op | source)
XLA Modules:
  0.0 23.8 jit_solution(6765608217849537428)
XLA Ops:
  0.7 21.4 %shard_map.46 = f32[4,2,32,256]{3,2,1,0:T(8,128)} custom-call(f32[8,32,256]{2,1,0:T(8,128)} %bitcast.8, f32[2,32,256]{2,1,0:T(8,128)} %bitcast.9, f32[1,3,4,15]{3,2,1,0:T(4,128)} %taps_ref.1, f32[1,1]{1,0:T(1,128)} %bitcast.7.back_ref), custom_call_target="tpu_custom_call" | custom-call | tf_op jit(solution)/shard_map/pallas_call | solution.py:261
  22.1 0.0 copy-start
  22.1 1.0 %reduce_sum.9 = f32[2,32,256]{2,1,0:T(8,128)S(1)} reduce(f32[4,2,32,256]{3,2,1,0:T(8,128)} %shard_map.46, f32[]{:T(128)} %constant.0.clone.1), dimensions={0}, to_apply=%region_0.0 | reduce | flops 49152 | bytes 327684 | tf_op jit(solution)/shard_map/reduce_sum | solution.py:296
  23.1 0.0 copy-done
  23.1 0.6 %fusion = f32[2,1,32,256]{3,2,1,0:T(8,128)} fusion(f32[2,1,32,256]{3,2,1,0:T(8,128)S(1)} %copy-done, f32[2,32,256]{2,1,0:T(8,128)S(1)} %reduce_sum.9), kind=kLoop, calls=%fused_computation.1 | loop fusion | flops 32768 | bytes 196608 | tf_op jit(solution)/shard_map/mul | solution.py:296
Async XLA Ops:
  22.1 1.0 %copy-start = (f32[2,1,32,256]{3,2,1,0:T(8,128)S(1)}, f32[2,1,32,256]{3,2,1,0:T(8,128)}, u32[]{:S(2)}) copy-start(f32[2,1,32,256]{3,2,1,0:T(8,128)} %param.5) | copy-start | bytes 196612
